TPU v7x, 1024 devices: a whole 4x8x16 slice. The times are simulated.
1024 devices in a mesh: inner: 16 (over z_lo, core), outer: 64 (over x, y, z_hi).
Axes of the slice: x: 4, y: 8, z: 16 (z_hi: 2, z_lo: 8; z = z_hi * 8 + z_lo), core: 2. Of those that a mesh axis runs over, the one named last changes fastest.
Arguments:
- tokens: bfloat16 [131072, 4096], P(('inner', 'outer')), may hold values from -24 to 24
- weight_codes: bfloat16 [4096, 512], P('inner'), may hold values from -127 to 127
- scales: float32 [1024], P('inner'), may hold values from 0.00012 to 0.0004
- cotangent: bfloat16 [131072, 512], P(('inner', 'outer')), may hold values from -6 to 6
Outputs:
- keys: bfloat16 [131072, 512], P(('inner', 'outer'))
- grad_tokens: bfloat16 [131072, 4096], P(('inner', 'outer'))
- grad_weight: float32 [4096, 512], P(('inner', 'outer'))
All inputs are finite; a program needn't handle non-finite values.
Results may differ from a plain program's by a relative error of at most 0.017.
Values may be sent and summed in bfloat16 or wider, within the bound.
A program may use at most 64 MiB of HBM per device.

v0:
```python
import jax
import jax.numpy as jnp
from jax import lax
from jax.sharding import PartitionSpec as P

EPS = 1e-05


def laid_out(blocks, dim):
    blocks = jnp.moveaxis(blocks, 0, dim)
    shape = blocks.shape
    return blocks.reshape(*shape[:dim], shape[dim] * shape[dim + 1], *shape[dim + 2 :])


def sent_to_all(shard, axis):
    count = lax.axis_size(axis)
    return lax.all_to_all(
        jnp.broadcast_to(shard[None], (count, *shard.shape)), axis, 0, 0, tiled=True
    )


def gather_directly(shard, axis, dim):
    return laid_out(sent_to_all(shard, axis), dim)


def in_blocks(shard, dim, count):
    shape = shard.shape
    blocks = shard.reshape(*shape[:dim], count, shape[dim] // count, *shape[dim + 1 :])
    return jnp.moveaxis(blocks, dim, 0)


def sum_at_owner(shard, axis, dim):
    blocks = in_blocks(shard, dim, lax.axis_size(axis))
    arrived = lax.all_to_all(blocks, axis, split_axis=0, concat_axis=0, tiled=True)
    return arrived.sum(axis=0)


def local(tokens, weight_codes, scales, cotangent):
    kv_width = cotangent.shape[1]
    block_rows = weight_codes.shape[0] // scales.shape[0]
    xf = tokens.astype(jnp.float32)
    inv_norm = lax.rsqrt(jnp.mean(xf * xf, axis=-1, keepdims=True) + EPS)
    normed_f = xf * inv_norm
    normed = normed_f.astype(jnp.bfloat16)
    packed = weight_codes.reshape(scales.shape[0], block_rows * kv_width)
    all_scales = gather_directly(scales, "inner", 0)
    code_piece = lax.all_gather(packed, "inner", axis=0, tiled=True)
    count_rows = code_piece.shape[0] * block_rows
    dequant = (code_piece.astype(jnp.float32) * all_scales[:, None]).reshape(count_rows, kv_width)
    dequant = dequant.astype(jnp.bfloat16)
    columns = normed
    key_total = jnp.dot(columns, dequant, preferred_element_type=jnp.float32)
    grad_piece = lax.dot_general(
        cotangent, dequant, (((1,), (1,)), ((), ())), preferred_element_type=jnp.float32
    )
    grad_normed = grad_piece
    key_total, grad_normed = (key_total, grad_normed)
    columns = normed
    product = lax.dot_general(
        columns, cotangent, (((0,), (0,)), ((), ())), preferred_element_type=jnp.float32
    )
    group_sum = lax.psum_scatter(
        lax.optimization_barrier(product.astype(jnp.bfloat16))
        .astype(jnp.float32)
        .astype(jnp.bfloat16),
        "inner",
        scatter_dimension=0,
        tiled=True,
    ).astype(jnp.float32)
    grad_weight = sum_at_owner(group_sum, "outer", 0)
    keys = key_total.astype(jnp.bfloat16)
    inner_mean = jnp.mean(grad_normed * normed_f, axis=-1, keepdims=True)
    grad_tokens = (inv_norm * (grad_normed - normed_f * inner_mean)).astype(jnp.bfloat16)
    return (keys, grad_tokens, grad_weight)


def solution(mesh):
    in_specs = (
        P(("inner", "outer"), None),
        P("inner", None),
        P("inner"),
        P(("inner", "outer"), None),
    )
    out_specs = (
        P(("inner", "outer"), None),
        P(("inner", "outer"), None),
        P(("inner", "outer"), None),
    )
    return jax.shard_map(local, mesh=mesh, in_specs=in_specs, out_specs=out_specs, check_vma=False)
```

profile of v0, /device:TPU:6, one launch (start us, length us, event | category | flops | bytes accessed | tf_op | source)
XLA Modules:
  0.0 279.4 jit_solution(8972979471129071439)
XLA Ops:
  7.2 0.0 reduce-scatter.2.cloned.1.call-start
  7.2 1.6 copy.7
  8.9 0.6 fusion.7
  9.4 3.2 %convolution_convert_fusion = bf16[4096,512]{1,0:T(8,128)(2,1)} fusion(bf16[128,512]{1,0:T(8,128)(2,1)S(1)} %copy-done, bf16[128,4096]{0,1:T(8,128)(2,1)S(1)} %copy.7, f32[128]{0:T(128)S(1)} %add_rsqrt_fusion), kind=kOutput, calls=%fused_computation.1 | convolution fusion | flops 540540928 | bytes 5374464 | tf_op jit(solution)/shard_map/dot_general | solution.py:59
  12.7 0.0 reduce-scatter.2.cloned.1.call-update
  12.7 0.0 all-gather.2.cloned.1.call-start
  12.7 0.9 copy-done.1
  13.6 0.9 reshape.37
  14.5 0.0 all-gather.2.cloned.1.call-update
  14.5 26.0 %all_to_all.11 = f32[16,1,64]{2,1,0:T(1,128)S(1)} all-to-all(f32[16,1,64]{2,1,0:T(1,128)S(1)} %broadcast_in_dim.2), channel_id=1, replica_groups=mesh['inner'=16,'outer'=64] {'inner'}, dimensions={0} | all-to-all | bytes 8192 | tf_op jit(solution)/shard_map/all_to_all | solution.py:17
  40.5 0.5 broadcast.29
  41.0 0.7 reduce.3
  41.7 0.1 mul.41
  41.8 97.7 %reduce-scatter.2.cloned.1.call-done = bf16[256,512]{1,0:T(8,128)(2,1)} async-done(((bf16[4096,512]{1,0:T(8,128)(2,1)}), bf16[256,512]{1,0:T(8,128)(2,1)}) %reduce-scatter.2.cloned.1.call-update) | async-done | bytes 262160 | tf_op jit(solution)/shard_map/reduce_scatter | solution.py:62
  139.5 2.0 reshape.41
  141.5 17.8 %all-to-all-start.1 = ((f32[64,4,512]{2,1,0:T(4,128)}), f32[64,4,512]{2,1,0:T(4,128)S(1)}, u32[]{:S(2)}, u32[]{:S(2)}) async-start(f32[64,4,512]{2,1,0:T(4,128)} %reshape.41), calls=%async_computation.2 | async-start | bytes 1048576 | tf_op jit(solution)/shard_map/all_to_all | solution.py:34
  159.2 91.3 %all-gather.2.cloned.1.call-done = bf16[1024,2048]{1,0:T(8,128)(2,1)} async-done(((bf16[64,2048]{1,0:T(8,128)(2,1)}), bf16[1024,2048]{1,0:T(8,128)(2,1)}) %all-gather.2.cloned.1.call-update) | async-done | bytes 4194320 | tf_op jit(solution)/shard_map/all_gather | solution.py:47
  250.6 4.9 %multiply_convert_fusion = bf16[1024,2048]{1,0:T(8,128)(2,1)} fusion(bf16[1024,2048]{1,0:T(8,128)(2,1)} %all-gather.2.cloned.1.call-done, f32[1024]{0:T(1024)S(1)} %mul.41), kind=kLoop, calls=%fused_computation | loop fusion | flops 6291456 | bytes 8392704 | tf_op jit(solution)/shard_map/convert_element_type | solution.py:50
  255.5 7.5 %convert_element_type.31 = bf16[4096,512]{1,0:T(8,128)(2,1)} reshape(bf16[1024,2048]{1,0:T(8,128)(2,1)} %multiply_convert_fusion) | data formatting | bytes 8388608 | tf_op jit(solution)/shard_map/convert_element_type | solution.py:50
  263.0 3.5 %fusion.3 = (f32[128]{0:T(128)S(1)}, f32[128,4096]{0,1:T(8,128)S(1)}) fusion(bf16[128,4096]{0,1:T(8,128)(2,1)S(1)} %copy.7, f32[128]{0:T(128)S(1)} %add_rsqrt_fusion, bf16[4096,512]{1,0:T(8,128)(2,1)} %convert_element_type.31, bf16[128,512]{1,0:T(8,128)(2,1)S(1)} %copy-done), kind=kOutput, calls=%fused_computation.8 | convolution fusion | flops 538967936 | bytes 7472128 | tf_op jit(solution)/shard_map/dot_general | solution.py:53
  266.5 0.4 fusion.6
  266.9 1.3 copy.8
  268.2 3.6 %convolution_convert_fusion.1 = bf16[128,512]{1,0:T(8,128)(2,1)} fusion(bf16[4096,512]{1,0:T(8,128)(2,1)} %convert_element_type.31, bf16[128,4096]{0,1:T(8,128)(2,1)S(1)} %copy.7, f32[128]{0:T(128)S(1)} %add_rsqrt_fusion), kind=kOutput, calls=%fused_computation.13 | convolution fusion | flops 538509312 | bytes 5374464 | tf_op jit(solution)/shard_map/dot_general | solution.py:52
  271.8 0.7 reduce_sum.29
  (9 shorter events, 0.0 us)
Async XLA Ops:
  7.2 2.3 copy-start
  7.2 132.3 %reduce-scatter.2.cloned.1.call-start = ((), (), s32[]{:S(2)}) async-start(), calls=%async_computation.4 | async-start | bytes 4456448 | tf_op jit(solution)/shard_map/reduce_scatter | solution.py:62
  12.7 0.9 copy-start.1
  12.7 1.8 copy-start.2
  12.7 237.9 %all-gather.2.cloned.1.call-start = ((), (), s32[]{:S(2)}) async-start(), calls=%async_computation.3 | async-start | bytes 4456448 | tf_op jit(solution)/shard_map/all_gather | solution.py:47
  141.5 130.4 %all-to-all-start.1 = ((f32[64,4,512]{2,1,0:T(4,128)}), f32[64,4,512]{2,1,0:T(4,128)S(1)}, u32[]{:S(2)}, u32[]{:S(2)}) async-start(f32[64,4,512]{2,1,0:T(4,128)} %reshape.41), calls=%async_computation.2 | async-start | bytes 1048576 | tf_op jit(solution)/shard_map/all_to_all | solution.py:34
Sparse Core Ops, SparseCore 0:
  12.8 126.6 reduce-scatter.1
  142.7 107.8 all-gather.1
where the time goes:
time: 280 us; the launch traced here: 279 us
  waiting for transfers between devices  189 us (68%)
  blocking collectives  26 us (9%)
  starting transfers between devices  17.9 us (6%)
  local copies, waits for them, and re-layouts  14.8 us (5%)
  between operations  14.1 us (5%)
  matrix products  10.3 us (4%)
  other arithmetic  7.26 us (3%)
    reduce_scatter x1, waiting for transfers between devices, local(): lax.psum_scatter(lax.optimization_barrier(product.astype(jnp.bfloat16)).a...  97.7 us
    all_gather x1, waiting for transfers between devices, local(): code_piece = lax.all_gather(packed, 'inner', axis=0, tiled=True)  91.3 us
    all_to_all x1, blocking collectives, sent_to_all(): lax.all_to_all(jnp.broadcast_to(shard[None], (count, *shard.shape)), axis...  26 us
    all_to_all x1, starting transfers between devices, sum_at_owner(): lax.all_to_all(blocks, axis, split_axis=0, concat_axis=0, tiled=True)  17.8 us
    convert_element_type x1, local copies, waits for them, and re-layouts, local(): dequant = dequant.astype(jnp.bfloat16)  7.54 us
  transfers between devices with their start and end apart: 3, of which 2 were waited for; matrix products, arithmetic and copies ran while one was open for 9% of the time, Pallas kernels for 0%

commit v1 on v0

v1 whole, which is shorter than its diff:
```python
import jax
import jax.numpy as jnp
from jax import lax
from jax.experimental import pallas as pl
from jax.experimental.pallas import tpu as pltpu
from jax.sharding import PartitionSpec as P

EPS = 1e-05
NX, NY, NZL, NZ = 4, 8, 8, 16
TOK, D, KV = 128, 4096, 512
ROWS = 256
HALF = ROWS // 2
LANE = 128
N_SEM = 96
MESH = pl.DeviceIdType.MESH
F32, BF16 = jnp.float32, jnp.bfloat16


def kernel(
    tok, codes, scales, cot, keys, grad_tokens, grad_weight,
    inv, nb, pair_n, pair_c, part, wbuf, gn, gt, kacc, macc,
    ys, yr, xs, xr, ra, rb, xds, xdr, yds, ydr, fin, zf, zs, zr,
    send_sem, recv_sem, out_sem, near, far,
):
    inner, outer = lax.axis_index("inner"), lax.axis_index("outer")
    c, zl = lax.rem(inner, 2), lax.div(inner, 2)
    zh, y, x = lax.rem(outer, 2), lax.rem(lax.div(outer, 2), NY), lax.div(outer, 2 * NY)
    z = zh * NZL + zl

    def at(nx, ny, nz, nc):
        return (lax.rem(nz, NZL) * 2 + nc, (nx * NY + ny) * 2 + lax.div(nz, NZL))

    def x_off(d):
        return lax.rem(x + d + NX, NX)

    def y_off(d):
        return lax.rem(y + d + NY, NY)

    def z_off(d):
        return lax.rem(z + d + NZ, NZ)

    def on_x(d):
        return at(x_off(d), y, z, c)

    def on_y(d):
        return at(x, y_off(d), z, c)

    def on_z(d):
        return at(x, y, z_off(d), c)

    partner = at(x, y, z, 1 - c)
    copies = []

    def send(src, dst, device):
        n = len(copies)
        copy = pltpu.make_async_remote_copy(
            src_ref=src, dst_ref=dst, send_sem=send_sem.at[n], recv_sem=recv_sem.at[n],
            device_id=device, device_id_type=MESH,
        )
        copy.start()
        copies.append(copy)
        return copy

    barrier = pltpu.get_barrier_semaphore()
    for device in (partner, on_z(1), on_z(-1), on_y(1), on_y(-1), on_x(1), on_x(-1)):
        pl.semaphore_signal(barrier, inc=1, device_id=device, device_id_type=MESH)

    groups = scales.shape[1]
    row = lax.broadcasted_iota(jnp.int32, (ROWS, groups), 0)
    col = lax.broadcasted_iota(jnp.int32, (ROWS, groups), 1)
    per_row = jnp.where(lax.div(row, ROWS // groups) == col, scales[...], 0.0)
    per_row = jnp.sum(per_row, axis=1, keepdims=True)
    wbuf[0, c] = (codes[...].astype(F32) * per_row).astype(BF16)

    pl.semaphore_wait(barrier, 7)

    got = {}

    def slot_of(way, k):
        return k if way > 0 or k in (0, 4) else 4 + k

    def rows_of(h):
        return pl.ds(h * HALF, HALF)

    def pass_on(way, k, h):
        got[way, k + 1, h] = send(
            wbuf.at[slot_of(way, k), c, rows_of(h)],
            wbuf.at[slot_of(way, k + 1), c, rows_of(h)],
            on_z(way),
        )

    def relay(slot, h):
        got["relay", slot, h] = send(
            wbuf.at[slot, c, rows_of(h)], wbuf.at[slot, c, rows_of(h)], partner
        )

    def arrive(way, k, h):
        got[way, k, h].wait_recv()
        if k < 3 or (k == 3 and h == (0 if way > 0 else 1)):
            pass_on(way, k, h)
        relay(slot_of(way, k), h)

    pass_on(1, 0, 0)
    pass_on(-1, 0, 1)
    pass_on(1, 0, 1)
    pass_on(-1, 0, 0)
    relay(0, 0)
    relay(0, 1)
    for d in (1, -1):
        pl.semaphore_signal(near.at[0], inc=1, device_id=on_y(d), device_id_type=MESH)

    total = jnp.zeros((TOK, LANE), F32)
    for k in range(D // LANE):
        v = tok[:, k * LANE : (k + 1) * LANE].astype(F32)
        total = total + v * v
    mean = jnp.sum(total, axis=1, keepdims=True) * (1.0 / D)
    inv[...] = jnp.broadcast_to(lax.rsqrt(mean + EPS), (TOK, LANE))
    for k in range(D // LANE):
        v = (tok[:, k * LANE : (k + 1) * LANE].astype(F32) * inv[...]).astype(BF16)
        strip = k // 2
        nb[strip % 2, strip // 2, :, (k % 2) * LANE : (k % 2 + 1) * LANE] = v

    n_copy = send(nb.at[1 - c], pair_n.at[:, pl.ds(TOK, TOK)], partner)
    c_copy = send(cot, pair_c.at[pl.ds(TOK, TOK)], partner)
    pair_c[:TOK] = cot[...]
    pair_n[:, :TOK] = nb[c]
    pl.semaphore_wait(near.at[0], 2)
    for d in (2, -2):
        pl.semaphore_signal(near.at[1], inc=1, device_id=on_y(d), device_id_type=MESH)
    c_copy.wait_recv()
    n_copy.wait_recv()

    def part_rows(b, _):
        p = lax.dot_general(
            pair_n[b], pair_c[...], (((0,), (0,)), ((), ())), preferred_element_type=F32
        )
        part[b] = p.reshape(NX, NY, 8, KV)
        return _

    lax.fori_loop(0, NZL, part_rows, 0)

    def lanes(color, j):
        return slice((color * 2 + j) * LANE, (color * 2 + j + 1) * LANE)

    def y_part(d, j):
        return part[:, :, y_off(d), :, lanes(0, j)].reshape(NZL * NX * 8, LANE)

    def x_part(d, j):
        return part[:, x_off(d), :, :, lanes(1, j)].reshape(NZL * NY * 8, LANE)

    ring = {}

    def hop(axis, way, j, s):
        n, mine, out, into, on = (
            (NY, y_part, ys, yr, on_y) if axis == "y" else (NX, x_part, xs, xr, on_x)
        )
        last = n // 2
        w = 0 if way > 0 else 1
        first = 1 if j == w else 2
        v = mine(way * (last + 1 - s), j)
        if s > first:
            ring[axis, way, j, s - 1].wait_recv()
            v = v + into[w, j, s - 2].astype(F32)
        out[w, j, s - 1] = v.astype(BF16)
        ring[axis, way, j, s] = send(out.at[w, j, s - 1], into.at[w, j, s - 1], on(way))

    def ring_sum(axis, j):
        n, mine, into = (NY, y_part, yr) if axis == "y" else (NX, x_part, xr)
        v = mine(0, j)
        for w, way in enumerate((1, -1)):
            ring[axis, way, j, n // 2].wait_recv()
            v = v + into[w, j, n // 2 - 1].astype(F32)
        return v

    def y_ring_end():
        for j in range(2):
            ra[:, :, :, j * LANE : (j + 1) * LANE] = ring_sum("y", j).reshape(NZL, NX, 8, LANE)

    def x_ring_end():
        for j in range(2):
            rb[:, :, :, j * LANE : (j + 1) * LANE] = ring_sum("x", j).reshape(NZL, NY, 8, LANE)

    direct = {}

    def x_direct():
        for d in range(1, NX):
            xds[d - 1] = ra[:, x_off(d)].reshape(NZL * 8, 2 * LANE).astype(BF16)
            direct["x", d] = send(xds.at[d - 1], xdr.at[d - 1], on_x(d))

    def x_direct_end():
        v = ra[:, x].reshape(NZL * 8, 2 * LANE)
        for d in range(1, NX):
            direct["x", d].wait_recv()
            v = v + xdr[d - 1].astype(F32)
        fin[:, :, : 2 * LANE] = v.reshape(NZL, 8, 2 * LANE)

    def y_direct():
        pl.semaphore_wait(near.at[1], 2)
        for d in range(1, NY):
            yds[d - 1] = rb[:, y_off(d)].reshape(NZL * 8, 2 * LANE).astype(BF16)
            direct["y", d] = send(yds.at[d - 1], ydr.at[d - 1], on_y(d))

    def y_direct_end():
        v = rb[:, y].reshape(NZL * 8, 2 * LANE)
        for d in range(1, NY):
            direct["y", d].wait_recv()
            v = v + ydr[d - 1].astype(F32)
        fin[:, :, 2 * LANE :] = v.reshape(NZL, 8, 2 * LANE)

    def z_direct():
        for h in range(2):
            v = jnp.concatenate(
                [fin[:, h * 4 : h * 4 + 4, k * LANE : (k + 1) * LANE] for k in range(4)], axis=1
            )
            zf[h] = v
            zs[h] = v.astype(BF16)
        pl.semaphore_wait(far.at[0], 1)
        pl.semaphore_wait(far.at[1], 1)
        for d in range(1, NZ):
            to = z_off(d)
            direct["z", d] = send(
                zs.at[lax.div(to, NZL), lax.rem(to, NZL)], zr.at[d - 1], on_z(d)
            )

    def z_direct_end():
        v = zf[zh, zl]
        for d in range(1, NZ):
            direct["z", d].wait_recv()
            v = v + zr[d - 1].astype(F32)
        for k in range(4):
            grad_weight[:, k * LANE : (k + 1) * LANE] = v[k * 4 : k * 4 + 4]

    kacc[...] = jnp.zeros_like(kacc)
    macc[...] = jnp.zeros_like(macc)

    def chip_of(slot):
        return lax.rem(zl + (NZL - slot if slot < 4 else slot if slot == 4 else slot - 4), NZL)

    def use(slot):
        b = chip_of(slot)
        for h in range(2):
            got["relay", slot, h].wait_recv()
        for p in range(2):
            w = wbuf[slot, p]
            kacc[...] += jnp.dot(nb[p, b], w, preferred_element_type=F32)
            g = lax.dot_general(
                cot[...], w, (((1,), (1,)), ((), ())), preferred_element_type=F32
            )
            gn[b, :, p * ROWS : (p + 1) * ROWS] = g
            for q in range(2):
                off = pl.multiple_of(b * (2 * ROWS) + (p * 2 + q) * LANE, LANE)
                nf = tok[:, pl.ds(off, LANE)].astype(F32) * inv[...]
                macc[...] += g[:, q * LANE : (q + 1) * LANE] * nf

    out_copies = []

    def finish_tokens():
        keys[...] = kacc[...].astype(BF16)
        inner_mean = jnp.sum(macc[...], axis=1, keepdims=True) * (1.0 / D)
        macc[...] = jnp.broadcast_to(inner_mean, (TOK, LANE))

        def strip(b, _):
            for q in range(4):
                off = pl.multiple_of(b * (4 * LANE) + q * LANE, LANE)
                nf = tok[:, pl.ds(off, LANE)].astype(F32) * inv[...]
                g = gn[b, :, q * LANE : (q + 1) * LANE]
                gt[:, pl.ds(off, LANE)] = (inv[...] * (g - nf * macc[...])).astype(BF16)
            return _

        lax.fori_loop(0, NZL, strip, 0)
        copy = pltpu.make_async_copy(gt, grad_tokens, out_sem)
        copy.start()
        out_copies.append(copy)

    def both(f, *args):
        k, first = args
        f(1, k, 0 if first else 1)
        f(-1, k, 1 if first else 0)

    def hops(axis, s, first):
        hop(axis, 1, 0 if first else 1, s)
        hop(axis, -1, 1 if first else 0, s)

    def far_signals():
        pl.semaphore_signal(far.at[0], inc=1, device_id=on_z(4), device_id_type=MESH)
        pl.semaphore_signal(far.at[1], inc=1, device_id=on_z(-4), device_id_type=MESH)

    hops("y", 1, True)
    hops("x", 1, True)
    hops("y", 2, False)
    hops("x", 2, False)
    both(arrive, 1, True)
    use(0)
    both(arrive, 1, False)
    hops("y", 2, True)
    both(arrive, 2, True)
    hops("y", 3, False)
    hops("x", 2, True)
    use(1)
    both(arrive, 2, False)
    hops("y", 3, True)
    hops("y", 4, False)
    use(5)
    both(arrive, 3, True)
    x_ring_end()
    y_direct()
    hops("y", 4, True)
    both(arrive, 3, False)
    use(2)
    use(6)
    y_ring_end()
    x_direct()
    both(arrive, 4, True)
    far_signals()
    use(3)
    use(7)
    use(4)
    x_direct_end()
    y_direct_end()
    z_direct()
    finish_tokens()
    z_direct_end()
    for copy in copies:
        copy.wait_send()
    for copy in out_copies:
        copy.wait()


def local(tokens, weight_codes, scales, cotangent):
    vmem = pl.BlockSpec(memory_space=pltpu.VMEM)
    return pl.pallas_call(
        kernel,
        out_shape=(
            jax.ShapeDtypeStruct((TOK, KV), BF16),
            jax.ShapeDtypeStruct((TOK, D), BF16),
            jax.ShapeDtypeStruct((4, KV), F32),
        ),
        in_specs=[vmem] * 4,
        out_specs=(vmem, pl.BlockSpec(memory_space=pl.ANY), vmem),
        scratch_shapes=[
            pltpu.VMEM((TOK, LANE), F32),
            pltpu.VMEM((2, NZL, TOK, ROWS), BF16),
            pltpu.VMEM((NZL, 2 * TOK, ROWS), BF16),
            pltpu.VMEM((2 * TOK, KV), BF16),
            pltpu.VMEM((NZL, NX, NY, 8, KV), F32),
            pltpu.VMEM((8, 2, ROWS, KV), BF16),
            pltpu.VMEM((NZL, TOK, 2 * ROWS), F32),
            pltpu.VMEM((TOK, D), BF16),
            pltpu.VMEM((TOK, KV), F32),
            pltpu.VMEM((TOK, LANE), F32),
            pltpu.VMEM((2, 2, NY // 2, NZL * NX * 8, LANE), BF16),
            pltpu.VMEM((2, 2, NY // 2, NZL * NX * 8, LANE), BF16),
            pltpu.VMEM((2, 2, NX // 2, NZL * NY * 8, LANE), BF16),
            pltpu.VMEM((2, 2, NX // 2, NZL * NY * 8, LANE), BF16),
            pltpu.VMEM((NZL, NX, 8, 2 * LANE), F32),
            pltpu.VMEM((NZL, NY, 8, 2 * LANE), F32),
            pltpu.VMEM((NX - 1, NZL * 8, 2 * LANE), BF16),
            pltpu.VMEM((NX - 1, NZL * 8, 2 * LANE), BF16),
            pltpu.VMEM((NY - 1, NZL * 8, 2 * LANE), BF16),
            pltpu.VMEM((NY - 1, NZL * 8, 2 * LANE), BF16),
            pltpu.VMEM((NZL, 8, KV), F32),
            pltpu.VMEM((2, NZL, 16, LANE), F32),
            pltpu.VMEM((2, NZL, 16, LANE), BF16),
            pltpu.VMEM((NZ - 1, 16, LANE), BF16),
            pltpu.SemaphoreType.DMA((N_SEM,)),
            pltpu.SemaphoreType.DMA((N_SEM,)),
            pltpu.SemaphoreType.DMA,
            pltpu.SemaphoreType.REGULAR((2,)),
            pltpu.SemaphoreType.REGULAR((2,)),
        ],
        compiler_params=pltpu.CompilerParams(collective_id=0, has_side_effects=True),
        name="key_projection",
    )(tokens, weight_codes, scales.reshape(1, -1), cotangent)


def solution(mesh):
    in_specs = (
        P(("inner", "outer"), None),
        P("inner", None),
        P("inner"),
        P(("inner", "outer"), None),
    )
    out_specs = (P(("inner", "outer"), None),) * 3
    return jax.shard_map(local, mesh=mesh, in_specs=in_specs, out_specs=out_specs, check_vma=False)
```

time: 280 us -> 63.8 us (0.23)
  waiting for transfers between devices: 189 us -> 0 us
  Pallas kernels: 0 us -> 57.6 us
  blocking collectives: 26 us -> 0 us
  starting transfers between devices: 17.9 us -> 0 us
  between operations: 14.1 us -> 0.64 us
  local copies, waits for them, and re-layouts: 14.8 us -> 4.47 us
  matrix products: 10.3 us -> 0 us
  other arithmetic: 7.26 us -> 0 us
    reduce_scatter x1 -> x0, waiting for transfers between devices: 97.7 us -> none  [local(): lax.psum_scatter(lax.optimization_barrier(product.astype(jnp.bfloat16)).a...]
    all_gather x1 -> x0, waiting for transfers between devices: 91.3 us -> none  [local(): code_piece = lax.all_gather(packed, 'inner', axis=0, tiled=True)]
    pallas_call x0 -> x1, Pallas kernels: none -> 57.6 us  [local(): pl.pallas_call(kernel, out_shape=(jax.ShapeDtypeStruct((TOK, KV), BF16),...]
    all_to_all x1 -> x0, blocking collectives: 26 us -> none  [sent_to_all(): lax.all_to_all(jnp.broadcast_to(shard[None], (count, *shard.shape)), axis...]
    all_to_all x1 -> x0, starting transfers between devices: 17.8 us -> none  [sum_at_owner(): lax.all_to_all(blocks, axis, split_axis=0, concat_axis=0, tiled=True)]
    dot_general x3 -> x0, matrix products: 10.3 us -> none  [the longest x1 3.6 us: local(): key_total = jnp.dot(columns, dequant, preferred_element_type=jnp.float32)]
    convert_element_type x1 -> x0, local copies, waits for them, and re-layouts: 7.54 us -> none  [local(): dequant = dequant.astype(jnp.bfloat16)]
    convert_element_type x2 -> x0, other arithmetic: 5.31 us -> none  [the longest x1 4.9 us: local(): dequant = dequant.astype(jnp.bfloat16)]
  transfers between devices with their start and end apart: 3 -> 0, of which waited for: 2 -> 0; matrix products, arithmetic and copies ran while one was open for 9% -> 0% of each run, Pallas kernels for 0% -> 0%
where the time goes in v1:
time: 63.8 us; the launch traced here: 62.7 us
  Pallas kernels  57.6 us (90%)
  local copies, waits for them, and re-layouts  4.47 us (7%)
  between operations  0.64 us (1%)
    pallas_call x1, Pallas kernels, local(): pl.pallas_call(kernel, out_shape=(jax.ShapeDtypeStruct((TOK, KV), BF16),...  57.6 us
    unnamed x5, local copies, waits for them, and re-layouts  4.47 us

profile of v1, /device:TPU:6, one launch (start us, length us, event | category | flops | bytes accessed | tf_op | source)
XLA Modules:
  0.0 62.7 jit_solution(13769584073908721614)
XLA Ops:
  0.6 57.6 %key_projection.1 = (bf16[128,512]{1,0:T(8,128)(2,1)}, bf16[128,4096]{1,0:T(8,128)(2,1)}, f32[4,512]{1,0:T(4,128)}) custom-call(bf16[128,4096]{1,0:T(8,128)(2,1)} %tok.1, bf16[256,512]{1,0:T(8,128)(2,1)} %codes.1, f32[1,64]{1,0:T(1,128)} %bitcast.1, bf16[128,512]{1,0:T(8,128)(2,1)} %cot.1), custom_call_target="tpu_custom_call" | custom-call | tf_op jit(solution)/shard_map/key_projection/pallas_call | solution.py:331
  58.2 1.6 %copy.10 = bf16[128,512]{1,0:T(8,128)(2,1)} copy(bf16[128,512]{1,0:T(8,128)(2,1)} %get-tuple-element.6) | data formatting | bytes 262144
  59.8 0.0 copy-start
  59.8 2.3 %copy.11 = bf16[128,4096]{1,0:T(8,128)(2,1)} copy(bf16[128,4096]{1,0:T(8,128)(2,1)} %get-tuple-element.7) | data formatting | bytes 2097152
  62.1 0.0 copy-done
  62.1 0.6 copy.12
Async XLA Ops:
  59.8 2.3 %copy-start = (f32[4,512]{1,0:T(4,128)S(1)}, f32[4,512]{1,0:T(4,128)}, u32[]{:S(2)}) copy-start(f32[4,512]{1,0:T(4,128)} %get-tuple-element.8) | copy-start | bytes 24580

commit v2 on v1

v2 whole, which is shorter than its diff:
```python
import jax
import jax.numpy as jnp
from jax import lax
from jax.experimental import pallas as pl
from jax.experimental.pallas import tpu as pltpu
from jax.sharding import PartitionSpec as P

EPS = 1e-05
NX, NY, NZL, NZ = 4, 8, 8, 16
TOK, D, KV = 128, 4096, 512
ROWS = 256
HALF = ROWS // 2
LANE = 128
N_SEM = 112
OUT = pltpu.VMEM
MESH = pl.DeviceIdType.MESH
F32, BF16 = jnp.float32, jnp.bfloat16


def kernel(
    tok_h, codes_h, scales_h, cot_h, keys, grad_tokens, grad_weight,
    tok, codes, scales, cot, inv, pair_n, pair_t, pair_c, part, wbuf, gn, kacc, macc,
    ys, yr, xs, xr, ra, rb, xds, xdr, yds, ydr, fin, zf, zs, zr,
    send_sem, recv_sem, in_sem, near, far,
):
    inner, outer = lax.axis_index("inner"), lax.axis_index("outer")
    c, zl = lax.rem(inner, 2), lax.div(inner, 2)
    zh, y, x = lax.rem(outer, 2), lax.rem(lax.div(outer, 2), NY), lax.div(outer, 2 * NY)
    z = zh * NZL + zl

    def at(nx, ny, nz, nc):
        return (lax.rem(nz, NZL) * 2 + nc, (nx * NY + ny) * 2 + lax.div(nz, NZL))

    def x_off(d):
        return lax.rem(x + d + NX, NX)

    def y_off(d):
        return lax.rem(y + d + NY, NY)

    def z_off(d):
        return lax.rem(z + d + NZ, NZ)

    def on_x(d):
        return at(x_off(d), y, z, c)

    def on_y(d):
        return at(x, y_off(d), z, c)

    def on_z(d):
        return at(x, y, z_off(d), c)

    partner = at(x, y, z, 1 - c)
    copies = []

    def send(src, dst, device):
        n = len(copies)
        copy = pltpu.make_async_remote_copy(
            src_ref=src, dst_ref=dst, send_sem=send_sem.at[n], recv_sem=recv_sem.at[n],
            device_id=device, device_id_type=MESH,
        )
        copy.start()
        copies.append(copy)
        return copy

    barrier = pltpu.get_barrier_semaphore()
    for device in (partner, on_z(1), on_z(-1), on_y(1), on_y(-1), on_x(1), on_x(-1)):
        pl.semaphore_signal(barrier, inc=1, device_id=device, device_id_type=MESH)

    loads = []

    def load(src, dst):
        copy = pltpu.make_async_copy(src, dst, in_sem.at[len(loads)])
        copy.start()
        loads.append(copy)
        return copy

    def strip_of(b, core):
        return pl.ds(pl.multiple_of(b * (2 * ROWS) + core * ROWS, ROWS), ROWS)

    load_s = load(scales_h, scales)
    load_w = load(codes_h, codes)
    load_t = [
        load(tok_h.at[:, pl.ds(k * 1024, 1024)], tok.at[:, pl.ds(k * 1024, 1024)]) for k in range(4)
    ]
    load_c = load(cot_h, cot)
    load_n = [load(tok_h.at[:, strip_of(b, c)], pair_n.at[b, pl.ds(0, TOK)]) for b in range(NZL)]

    load_s.wait()
    load_w.wait()
    groups = scales.shape[1]
    row = lax.broadcasted_iota(jnp.int32, (ROWS, groups), 0)
    col = lax.broadcasted_iota(jnp.int32, (ROWS, groups), 1)
    per_row = jnp.where(lax.div(row, ROWS // groups) == col, scales[...], 0.0)
    per_row = jnp.sum(per_row, axis=1, keepdims=True)
    wbuf[0, c] = (codes[...].astype(F32) * per_row).astype(BF16)

    pl.semaphore_wait(barrier, 7)

    n_copies = [
        send(tok_h.at[:, strip_of(b, 1 - c)], pair_n.at[b, pl.ds(TOK, TOK)], partner)
        for b in range(NZL)
    ]

    got = {}

    def slot_of(way, k):
        return k if way > 0 or k in (0, 4) else 4 + k

    def rows_of(h):
        return pl.ds(h * HALF, HALF)

    def pass_on(way, k, h):
        got[way, k + 1, h] = send(
            wbuf.at[slot_of(way, k), c, rows_of(h)],
            wbuf.at[slot_of(way, k + 1), c, rows_of(h)],
            on_z(way),
        )

    def relay(slot, h):
        got["relay", slot, h] = send(
            wbuf.at[slot, c, rows_of(h)], wbuf.at[slot, c, rows_of(h)], partner
        )

    def arrive(way, k, h):
        got[way, k, h].wait_recv()
        if k < 3 or (k == 3 and h == (0 if way > 0 else 1)):
            pass_on(way, k, h)
        relay(slot_of(way, k), h)

    pass_on(1, 0, 0)
    pass_on(-1, 0, 1)
    pass_on(1, 0, 1)
    pass_on(-1, 0, 0)
    relay(0, 0)
    relay(0, 1)
    for d in (1, -1):
        pl.semaphore_signal(near.at[0], inc=1, device_id=on_y(d), device_id_type=MESH)

    total = jnp.zeros((TOK, LANE), F32)
    for k in range(D // LANE):
        if k % 8 == 0:
            load_t[k // 8].wait()
        v = tok[:, k * LANE : (k + 1) * LANE].astype(F32)
        total = total + v * v
    mean = jnp.sum(total, axis=1, keepdims=True) * (1.0 / D)
    inv[...] = jnp.broadcast_to(lax.rsqrt(mean + EPS), (TOK, LANE))
    load_c.wait()
    for k in range(KV // LANE):
        lane = slice(k * LANE, (k + 1) * LANE)
        pair_c[:TOK, lane] = (cot[:, lane].astype(F32) * inv[...]).astype(BF16)
    c_copy = send(pair_c.at[pl.ds(0, TOK)], pair_c.at[pl.ds(TOK, TOK)], partner)

    for b in range(NZL):
        load_n[b].wait()
        n_copies[b].wait_recv()

    def turn(b, _):
        pair_t[b] = pair_n[b].T
        return _

    lax.fori_loop(0, NZL, turn, 0)
    pl.semaphore_wait(near.at[0], 2)
    for d in (2, -2):
        pl.semaphore_signal(near.at[1], inc=1, device_id=on_y(d), device_id_type=MESH)
    c_copy.wait_recv()

    def part_rows(color):
        lane = slice(color * 2 * LANE, (color + 1) * 2 * LANE)

        def rows(b, _):
            p = jnp.dot(pair_t[b], pair_c[:, lane], preferred_element_type=F32)
            part[b, :, :, :, lane] = p.reshape(NX, NY, 8, 2 * LANE)
            return _

        lax.fori_loop(0, NZL, rows, 0)

    def cut(color, q):
        lo = (color * 2 + q % 2) * LANE
        return slice(q // 2 * 4, q // 2 * 4 + 4), slice(lo, lo + LANE)

    def y_part(d, q):
        rows, lane = cut(0, q)
        return part[rows, :, y_off(d), :, lane].reshape(4 * NX * 8, LANE)

    def x_part(d, q):
        rows, lane = cut(1, q)
        return part[rows, x_off(d), :, :, lane].reshape(4 * NY * 8, LANE)

    ring = {}

    def hop(axis, way, q, s):
        n, mine, out, into, on = (
            (NY, y_part, ys, yr, on_y) if axis == "y" else (NX, x_part, xs, xr, on_x)
        )
        last = n // 2
        w = 0 if way > 0 else 1
        first = 1 if q // 2 == w else 2
        v = mine(way * (last + 1 - s), q)
        if s > first:
            ring[axis, way, q, s - 1].wait_recv()
            v = v + into[w, q, s - 2].astype(F32)
        out[w, q, s - 1] = v.astype(BF16)
        ring[axis, way, q, s] = send(out.at[w, q, s - 1], into.at[w, q, s - 1], on(way))

    def hops(axis, s, far_half):
        for k in range(2):
            hop(axis, 1, (0 if far_half else 2) + k, s)
            hop(axis, -1, (2 if far_half else 0) + k, s)

    def ring_sum(axis, q):
        n, mine, into = (NY, y_part, yr) if axis == "y" else (NX, x_part, xr)
        v = mine(0, q)
        for w, way in enumerate((1, -1)):
            ring[axis, way, q, n // 2].wait_recv()
            v = v + into[w, q, n // 2 - 1].astype(F32)
        return v

    def ring_end(axis):
        into, n = (ra, NX) if axis == "y" else (rb, NY)
        for q in (2, 0, 3, 1):
            lo = q % 2 * LANE
            into[q // 2 * 4 : q // 2 * 4 + 4, :, :, lo : lo + LANE] = ring_sum(axis, q).reshape(
                4, n, 8, LANE
            )

    direct = {}

    def x_direct():
        for d in (2, 1, 3):
            xds[d - 1] = ra[:, x_off(d)].reshape(NZL * 8, 2 * LANE).astype(BF16)
            direct["x", d] = send(xds.at[d - 1], xdr.at[d - 1], on_x(d))

    def x_direct_end():
        v = ra[:, x].reshape(NZL * 8, 2 * LANE)
        for d in (1, 3, 2):
            direct["x", d].wait_recv()
            v = v + xdr[d - 1].astype(F32)
        fin[:, :, : 2 * LANE] = v.reshape(NZL, 8, 2 * LANE)

    def y_direct():
        pl.semaphore_wait(near.at[1], 2)
        for d in (4, 3, 5, 2, 6, 1, 7):
            yds[d - 1] = rb[:, y_off(d)].reshape(NZL * 8, 2 * LANE).astype(BF16)
            direct["y", d] = send(yds.at[d - 1], ydr.at[d - 1], on_y(d))

    def y_direct_end():
        v = rb[:, y].reshape(NZL * 8, 2 * LANE)
        for d in range(1, NY):
            direct["y", d].wait_recv()
            v = v + ydr[d - 1].astype(F32)
        fin[:, :, 2 * LANE :] = v.reshape(NZL, 8, 2 * LANE)

    def z_direct():
        for h in range(2):
            v = jnp.concatenate(
                [fin[:, h * 4 : h * 4 + 4, k * LANE : (k + 1) * LANE] for k in range(4)], axis=1
            )
            zf[h] = v
            zs[h] = v.astype(BF16)
        pl.semaphore_wait(far.at[0], 1)
        pl.semaphore_wait(far.at[1], 1)
        for d in range(1, NZ):
            to = z_off(d)
            direct["z", d] = send(
                zs.at[lax.div(to, NZL), lax.rem(to, NZL)], zr.at[d - 1], on_z(d)
            )

    def z_direct_end():
        v = zf[zh, zl]
        for d in range(1, NZ):
            direct["z", d].wait_recv()
            v = v + zr[d - 1].astype(F32)
        for k in range(4):
            grad_weight[:, k * LANE : (k + 1) * LANE] = v[k * 4 : k * 4 + 4]

    kacc[...] = jnp.zeros_like(kacc)
    macc[...] = jnp.zeros_like(macc)

    def chip_of(slot):
        return lax.rem(zl + (NZL - slot if slot < 4 else slot if slot == 4 else slot - 4), NZL)

    def use(slot):
        b = chip_of(slot)
        for h in range(2):
            got["relay", slot, h].wait_recv()
        for p in range(2):
            w = wbuf[slot, p]
            t = tok[:, strip_of(b, p)]
            kacc[...] += jnp.dot(t, w, preferred_element_type=F32)
            g = lax.dot_general(
                cot[...], w, (((1,), (1,)), ((), ())), preferred_element_type=F32
            )
            gn[b, :, p * ROWS : (p + 1) * ROWS] = g
            gx = g * t.astype(F32)
            macc[...] += gx[:, :LANE] + gx[:, LANE:]

    def finish_tokens():
        for k in range(KV // LANE):
            lane = slice(k * LANE, (k + 1) * LANE)
            keys[:, lane] = (kacc[:, lane] * inv[...]).astype(BF16)
        inner_mean = jnp.sum(macc[...] * inv[...], axis=1, keepdims=True) * (1.0 / D)
        macc[...] = jnp.broadcast_to(inner_mean, (TOK, LANE))

        def strip(b, _):
            for q in range(4):
                off = pl.multiple_of(b * (4 * LANE) + q * LANE, LANE)
                nf = tok[:, pl.ds(off, LANE)].astype(F32) * inv[...]
                g = gn[b, :, q * LANE : (q + 1) * LANE]
                grad_tokens[:, pl.ds(off, LANE)] = (inv[...] * (g - nf * macc[...])).astype(BF16)
            return _

        lax.fori_loop(0, NZL, strip, 0)

    def both(k, first):
        arrive(1, k, 0 if first else 1)
        arrive(-1, k, 1 if first else 0)

    def far_signals():
        pl.semaphore_signal(far.at[0], inc=1, device_id=on_z(4), device_id_type=MESH)
        pl.semaphore_signal(far.at[1], inc=1, device_id=on_z(-4), device_id_type=MESH)

    part_rows(0)
    hops("y", 1, True)
    hops("y", 2, False)
    part_rows(1)
    hops("x", 1, True)
    hops("x", 2, False)
    both(1, True)
    hops("y", 2, True)
    both(1, False)
    hops("y", 3, False)
    use(0)
    hops("x", 2, True)
    both(2, True)
    hops("y", 3, True)
    hops("y", 4, False)
    both(2, False)
    use(1)
    hops("y", 4, True)
    both(3, True)
    ring_end("x")
    y_direct()
    ring_end("y")
    x_direct()
    both(3, False)
    use(5)
    use(2)
    both(4, True)
    far_signals()
    x_direct_end()
    use(6)
    y_direct_end()
    z_direct()
    use(3)
    use(7)
    use(4)
    finish_tokens()
    z_direct_end()
    for copy in copies:
        copy.wait_send()


def put_out(keys, grad_tokens, grad_weight, keys_h, grad_tokens_h, grad_weight_h, sem):
    pairs = ((grad_tokens, grad_tokens_h), (keys, keys_h), (grad_weight, grad_weight_h))
    copies = [pltpu.make_async_copy(a, b, sem.at[i]) for i, (a, b) in enumerate(pairs)]
    for copy in copies:
        copy.start()
    for copy in copies:
        copy.wait()


def local(tokens, weight_codes, scales, cotangent):
    vmem = pl.BlockSpec(memory_space=pltpu.VMEM)
    hbm = pl.BlockSpec(memory_space=pl.ANY)
    shapes = (((TOK, KV), BF16), ((TOK, D), BF16), ((4, KV), F32))
    out = pl.pallas_call(
        kernel,
        out_shape=tuple(OUT(*s) for s in shapes),
        in_specs=[pl.BlockSpec(memory_space=pltpu.HBM)] * 4,
        out_specs=(vmem,) * 3,
        scratch_shapes=[
            pltpu.VMEM((TOK, D), BF16),
            pltpu.VMEM((ROWS, KV), BF16),
            pltpu.VMEM((1, ROWS // 4), F32),
            pltpu.VMEM((TOK, KV), BF16),
            pltpu.VMEM((TOK, LANE), F32),
            pltpu.VMEM((NZL, 2 * TOK, ROWS), BF16),
            pltpu.VMEM((NZL, ROWS, 2 * TOK), BF16),
            pltpu.VMEM((2 * TOK, KV), BF16),
            pltpu.VMEM((NZL, NX, NY, 8, KV), F32),
            pltpu.VMEM((8, 2, ROWS, KV), BF16),
            pltpu.VMEM((NZL, TOK, 2 * ROWS), F32),
            pltpu.VMEM((TOK, KV), F32),
            pltpu.VMEM((TOK, LANE), F32),
            pltpu.VMEM((2, 4, NY // 2, 4 * NX * 8, LANE), BF16),
            pltpu.VMEM((2, 4, NY // 2, 4 * NX * 8, LANE), BF16),
            pltpu.VMEM((2, 4, NX // 2, 4 * NY * 8, LANE), BF16),
            pltpu.VMEM((2, 4, NX // 2, 4 * NY * 8, LANE), BF16),
            pltpu.VMEM((NZL, NX, 8, 2 * LANE), F32),
            pltpu.VMEM((NZL, NY, 8, 2 * LANE), F32),
            pltpu.VMEM((NX - 1, NZL * 8, 2 * LANE), BF16),
            pltpu.VMEM((NX - 1, NZL * 8, 2 * LANE), BF16),
            pltpu.VMEM((NY - 1, NZL * 8, 2 * LANE), BF16),
            pltpu.VMEM((NY - 1, NZL * 8, 2 * LANE), BF16),
            pltpu.VMEM((NZL, 8, KV), F32),
            pltpu.VMEM((2, NZL, 16, LANE), F32),
            pltpu.VMEM((2, NZL, 16, LANE), BF16),
            pltpu.VMEM((NZ - 1, 16, LANE), BF16),
            pltpu.SemaphoreType.DMA((N_SEM,)),
            pltpu.SemaphoreType.DMA((N_SEM,)),
            pltpu.SemaphoreType.DMA((16,)),
            pltpu.SemaphoreType.REGULAR((2,)),
            pltpu.SemaphoreType.REGULAR((2,)),
        ],
        compiler_params=pltpu.CompilerParams(
            collective_id=0, has_side_effects=True, vmem_limit_bytes=65_750_000
        ),
        name="key_projection",
    )(tokens, weight_codes, scales.reshape(1, -1), cotangent)
    return pl.pallas_call(
        put_out,
        out_shape=tuple(jax.ShapeDtypeStruct(*s) for s in shapes),
        in_specs=[vmem] * 3,
        out_specs=(hbm,) * 3,
        scratch_shapes=[pltpu.SemaphoreType.DMA((3,))],
        compiler_params=pltpu.CompilerParams(vmem_limit_bytes=16 << 20),
        name="put_out",
    )(*out)


def solution(mesh):
    in_specs = (
        P(("inner", "outer"), None),
        P("inner", None),
        P("inner"),
        P(("inner", "outer"), None),
    )
    out_specs = (P(("inner", "outer"), None),) * 3
    return jax.shard_map(local, mesh=mesh, in_specs=in_specs, out_specs=out_specs, check_vma=False)
```

time: 63.8 us -> 55.7 us (0.87)
  local copies, waits for them, and re-layouts: 4.47 us -> 0 us
  Pallas kernels: 57.6 us -> 54.4 us
    unnamed x5 -> x0, local copies, waits for them, and re-layouts: 4.47 us -> none
    pallas_call x1 -> x2, Pallas kernels: 57.6 us -> 54.4 us  [the longest x1 53.3 us: local(): pl.pallas_call(kernel, out_shape=tuple((OUT(*s) for s in shapes)), in_spe...]
where the time goes in v2:
time: 55.7 us; the launch traced here: 55 us
  Pallas kernels  54.4 us (98%)
  between operations  0.64 us (1%)
    pallas_call x1, Pallas kernels, local(): pl.pallas_call(kernel, out_shape=tuple((OUT(*s) for s in shapes)), in_spe...  53.3 us

profile of v2, /device:TPU:6, one launch (start us, length us, event | category | flops | bytes accessed | tf_op | source)
XLA Modules:
  0.0 55.0 jit_solution(14136515156230643611)
XLA Ops:
  0.6 53.3 %key_projection.1 = (bf16[128,512]{1,0:T(8,128)(2,1)S(1)}, bf16[128,4096]{1,0:T(8,128)(2,1)S(1)}, f32[4,512]{1,0:T(4,128)S(1)}) custom-call(bf16[128,4096]{1,0:T(8,128)(2,1)} %tok_h.1, bf16[256,512]{1,0:T(8,128)(2,1)} %codes_h.1, f32[1,64]{1,0:T(1,128)} %bitcast.1, bf16[128,512]{1,0:T(8,128)(2,1)} %cot_h.1), custom_call_target="tpu_custom_call" | custom-call | tf_op jit(solution)/shard_map/key_projection/pallas_call | solution.py:376
  54.0 1.0 %put_out.1 = (bf16[128,512]{1,0:T(8,128)(2,1)}, bf16[128,4096]{1,0:T(8,128)(2,1)}, f32[4,512]{1,0:T(4,128)}) custom-call(bf16[128,512]{1,0:T(8,128)(2,1)S(1)} %get-tuple-element.6.keys, bf16[128,4096]{1,0:T(8,128)(2,1)S(1)} %get-tuple-element.7.grad_tokens, f32[4,512]{1,0:T(4,128)S(1)} %get-tuple-element.8.grad_weight), custom_call_target="tpu_custom_call" | custom-call | tf_op jit(solution)/shard_map/put_out/pallas_call | solution.py:420

commit v3 on v2

--- a/solution.py
+++ b/solution.py
@@ -11,7 +11,7 @@
 ROWS = 256
 HALF = ROWS // 2
 LANE = 128
-N_SEM = 112
+N_SEM = 136
 OUT = pltpu.VMEM
 MESH = pl.DeviceIdType.MESH
 F32, BF16 = jnp.float32, jnp.bfloat16
@@ -19,9 +19,9 @@
 
 def kernel(
     tok_h, codes_h, scales_h, cot_h, keys, grad_tokens, grad_weight,
-    tok, codes, scales, cot, inv, pair_n, pair_t, pair_c, part, wbuf, gn, kacc, macc,
+    tok, codes, scales, cot, inv, cot_n, given, taken, part, wbuf, gn, kacc, macc,
     ys, yr, xs, xr, ra, rb, xds, xdr, yds, ydr, fin, zf, zs, zr,
-    send_sem, recv_sem, in_sem, near, far,
+    send_sem, recv_sem, in_sem, known,
 ):
     inner, outer = lax.axis_index("inner"), lax.axis_index("outer")
     c, zl = lax.rem(inner, 2), lax.div(inner, 2)
@@ -83,7 +83,6 @@
         load(tok_h.at[:, pl.ds(k * 1024, 1024)], tok.at[:, pl.ds(k * 1024, 1024)]) for k in range(4)
     ]
     load_c = load(cot_h, cot)
-    load_n = [load(tok_h.at[:, strip_of(b, c)], pair_n.at[b, pl.ds(0, TOK)]) for b in range(NZL)]
 
     load_s.wait()
     load_w.wait()
@@ -93,48 +92,6 @@
     per_row = jnp.where(lax.div(row, ROWS // groups) == col, scales[...], 0.0)
     per_row = jnp.sum(per_row, axis=1, keepdims=True)
     wbuf[0, c] = (codes[...].astype(F32) * per_row).astype(BF16)
-
-    pl.semaphore_wait(barrier, 7)
-
-    n_copies = [
-        send(tok_h.at[:, strip_of(b, 1 - c)], pair_n.at[b, pl.ds(TOK, TOK)], partner)
-        for b in range(NZL)
-    ]
-
-    got = {}
-
-    def slot_of(way, k):
-        return k if way > 0 or k in (0, 4) else 4 + k
-
-    def rows_of(h):
-        return pl.ds(h * HALF, HALF)
-
-    def pass_on(way, k, h):
-        got[way, k + 1, h] = send(
-            wbuf.at[slot_of(way, k), c, rows_of(h)],
-            wbuf.at[slot_of(way, k + 1), c, rows_of(h)],
-            on_z(way),
-        )
-
-    def relay(slot, h):
-        got["relay", slot, h] = send(
-            wbuf.at[slot, c, rows_of(h)], wbuf.at[slot, c, rows_of(h)], partner
-        )
-
-    def arrive(way, k, h):
-        got[way, k, h].wait_recv()
-        if k < 3 or (k == 3 and h == (0 if way > 0 else 1)):
-            pass_on(way, k, h)
-        relay(slot_of(way, k), h)
-
-    pass_on(1, 0, 0)
-    pass_on(-1, 0, 1)
-    pass_on(1, 0, 1)
-    pass_on(-1, 0, 0)
-    relay(0, 0)
-    relay(0, 1)
-    for d in (1, -1):
-        pl.semaphore_signal(near.at[0], inc=1, device_id=on_y(d), device_id_type=MESH)
 
     total = jnp.zeros((TOK, LANE), F32)
     for k in range(D // LANE):
@@ -147,32 +104,85 @@
     load_c.wait()
     for k in range(KV // LANE):
         lane = slice(k * LANE, (k + 1) * LANE)
-        pair_c[:TOK, lane] = (cot[:, lane].astype(F32) * inv[...]).astype(BF16)
-    c_copy = send(pair_c.at[pl.ds(0, TOK)], pair_c.at[pl.ds(TOK, TOK)], partner)
-
-    for b in range(NZL):
-        load_n[b].wait()
-        n_copies[b].wait_recv()
-
-    def turn(b, _):
-        pair_t[b] = pair_n[b].T
-        return _
-
-    lax.fori_loop(0, NZL, turn, 0)
-    pl.semaphore_wait(near.at[0], 2)
-    for d in (2, -2):
-        pl.semaphore_signal(near.at[1], inc=1, device_id=on_y(d), device_id_type=MESH)
-    c_copy.wait_recv()
-
-    def part_rows(color):
-        lane = slice(color * 2 * LANE, (color + 1) * 2 * LANE)
-
+        cot_n[:, lane] = (cot[:, lane].astype(F32) * inv[...]).astype(BF16)
+    pl.semaphore_wait(barrier, 7)
+
+    got = {}
+
+    def slot_of(way, k):
+        return k if way > 0 or k in (0, 4) else 4 + k
+
+    def rows_of(h):
+        return pl.ds(h * HALF, HALF)
+
+    def pass_on(way, k, h):
+        got[way, k + 1, h] = send(
+            wbuf.at[slot_of(way, k), c, rows_of(h)],
+            wbuf.at[slot_of(way, k + 1), c, rows_of(h)],
+            on_z(way),
+        )
+
+    def relay(slot, h):
+        got["relay", slot, h] = send(
+            wbuf.at[slot, c, rows_of(h)], wbuf.at[slot, c, rows_of(h)], partner
+        )
+
+    def arrive(way, k, h):
+        got[way, k, h].wait_recv()
+        if k < 3 or (k == 3 and h == (0 if way > 0 else 1)):
+            pass_on(way, k, h)
+        relay(slot_of(way, k), h)
+
+    pass_on(1, 0, 0)
+    pass_on(-1, 0, 1)
+    pass_on(1, 0, 1)
+    pass_on(-1, 0, 0)
+    for d in (1, -1):
+        pl.semaphore_signal(known.at[0], inc=1, device_id=on_y(d), device_id_type=MESH)
+        pl.semaphore_signal(known.at[0], inc=1, device_id=on_z(d), device_id_type=MESH)
+
+    def rows_for(core, store):
         def rows(b, _):
-            p = jnp.dot(pair_t[b], pair_c[:, lane], preferred_element_type=F32)
-            part[b, :, :, :, lane] = p.reshape(NX, NY, 8, 2 * LANE)
+            store(
+                b,
+                lax.dot_general(
+                    tok[:, strip_of(b, core)], cot_n[...], (((0,), (0,)), ((), ())),
+                    preferred_element_type=F32,
+                ).reshape(NX, NY, 8, KV),
+            )
             return _
 
-        lax.fori_loop(0, NZL, rows, 0)
+        lax.fori_loop(0, NZL, rows, 0, unroll=2)
+
+    def keep(b, v):
+        part[b] = v
+
+    def give(b, v):
+        given[b] = v.astype(BF16)
+
+    pairs = {}
+
+    def give_block(axis, d):
+        if axis == "y":
+            at_block = (slice(None), slice(None), y_off(d), slice(None), slice(0, 2 * LANE))
+        else:
+            at_block = (slice(None), x_off(d), slice(None), slice(None), slice(2 * LANE, KV))
+        pairs[axis, d] = send(given.at[at_block], taken.at[at_block], partner)
+
+    def need_block(axis, d):
+        copy = pairs.pop((axis, d % (NY if axis == "y" else NX)), None)
+        if copy is not None:
+            copy.wait_recv()
+
+    rows_for(1 - c, give)
+    for axis, d in (
+        ("x", 2), ("y", 4), ("x", 1), ("x", 3), ("y", 3), ("y", 5),
+        ("y", 2), ("y", 6), ("y", 1), ("y", 7), ("x", 0), ("y", 0),
+    ):
+        give_block(axis, d)
+    relay(0, 0)
+    relay(0, 1)
+    rows_for(c, keep)
 
     def cut(color, q):
         lo = (color * 2 + q % 2) * LANE
@@ -180,11 +190,15 @@
 
     def y_part(d, q):
         rows, lane = cut(0, q)
-        return part[rows, :, y_off(d), :, lane].reshape(4 * NX * 8, LANE)
+        need_block("y", d)
+        v = part[rows, :, y_off(d), :, lane] + taken[rows, :, y_off(d), :, lane].astype(F32)
+        return v.reshape(4 * NX * 8, LANE)
 
     def x_part(d, q):
         rows, lane = cut(1, q)
-        return part[rows, x_off(d), :, :, lane].reshape(4 * NY * 8, LANE)
+        need_block("x", d)
+        v = part[rows, x_off(d), :, :, lane] + taken[rows, x_off(d), :, :, lane].astype(F32)
+        return v.reshape(4 * NY * 8, LANE)
 
     ring = {}
 
@@ -238,7 +252,6 @@
         fin[:, :, : 2 * LANE] = v.reshape(NZL, 8, 2 * LANE)
 
     def y_direct():
-        pl.semaphore_wait(near.at[1], 2)
         for d in (4, 3, 5, 2, 6, 1, 7):
             yds[d - 1] = rb[:, y_off(d)].reshape(NZL * 8, 2 * LANE).astype(BF16)
             direct["y", d] = send(yds.at[d - 1], ydr.at[d - 1], on_y(d))
@@ -250,28 +263,29 @@
             v = v + ydr[d - 1].astype(F32)
         fin[:, :, 2 * LANE :] = v.reshape(NZL, 8, 2 * LANE)
 
-    def z_direct():
+    def z_direct(color):
+        lo = color * 2 * LANE
         for h in range(2):
             v = jnp.concatenate(
-                [fin[:, h * 4 : h * 4 + 4, k * LANE : (k + 1) * LANE] for k in range(4)], axis=1
+                [fin[:, h * 4 : h * 4 + 4, lo + k * LANE : lo + (k + 1) * LANE] for k in range(2)],
+                axis=1,
             )
-            zf[h] = v
-            zs[h] = v.astype(BF16)
-        pl.semaphore_wait(far.at[0], 1)
-        pl.semaphore_wait(far.at[1], 1)
+            zf[color, h] = v
+            zs[color, h] = v.astype(BF16)
         for d in range(1, NZ):
             to = z_off(d)
-            direct["z", d] = send(
-                zs.at[lax.div(to, NZL), lax.rem(to, NZL)], zr.at[d - 1], on_z(d)
+            direct["z", color, d] = send(
+                zs.at[color, lax.div(to, NZL), lax.rem(to, NZL)], zr.at[color, d - 1], on_z(d)
             )
 
-    def z_direct_end():
-        v = zf[zh, zl]
+    def z_direct_end(color):
+        v = zf[color, zh, zl]
         for d in range(1, NZ):
-            direct["z", d].wait_recv()
-            v = v + zr[d - 1].astype(F32)
-        for k in range(4):
-            grad_weight[:, k * LANE : (k + 1) * LANE] = v[k * 4 : k * 4 + 4]
+            direct["z", color, d].wait_recv()
+            v = v + zr[color, d - 1].astype(F32)
+        for k in range(2):
+            lo = (color * 2 + k) * LANE
+            grad_weight[:, lo : lo + LANE] = v[k * 4 : k * 4 + 4]
 
     kacc[...] = jnp.zeros_like(kacc)
     macc[...] = jnp.zeros_like(macc)
@@ -315,47 +329,53 @@
         arrive(1, k, 0 if first else 1)
         arrive(-1, k, 1 if first else 0)
 
-    def far_signals():
-        pl.semaphore_signal(far.at[0], inc=1, device_id=on_z(4), device_id_type=MESH)
-        pl.semaphore_signal(far.at[1], inc=1, device_id=on_z(-4), device_id_type=MESH)
-
-    part_rows(0)
+    def know(r):
+        pl.semaphore_wait(known.at[r], 4 if r < 2 else 2)
+        for d in (2 << r, -2 << r):
+            if r == 0:
+                pl.semaphore_signal(known.at[1], inc=1, device_id=on_y(d), device_id_type=MESH)
+            if r < 2:
+                pl.semaphore_signal(known.at[r + 1], inc=1, device_id=on_z(d), device_id_type=MESH)
+
+    hops("x", 1, True)
+    hops("x", 2, False)
     hops("y", 1, True)
     hops("y", 2, False)
-    part_rows(1)
-    hops("x", 1, True)
-    hops("x", 2, False)
+    know(0)
     both(1, True)
+    use(0)
     hops("y", 2, True)
     both(1, False)
+    hops("x", 2, True)
     hops("y", 3, False)
-    use(0)
-    hops("x", 2, True)
+    know(1)
+    hops("y", 3, True)
     both(2, True)
-    hops("y", 3, True)
     hops("y", 4, False)
+    use(1)
     both(2, False)
-    use(1)
     hops("y", 4, True)
-    both(3, True)
     ring_end("x")
     y_direct()
+    use(5)
+    use(2)
+    both(3, True)
     ring_end("y")
     x_direct()
+    know(2)
+    use(6)
+    x_direct_end()
+    z_direct(0)
     both(3, False)
-    use(5)
-    use(2)
+    y_direct_end()
+    z_direct(1)
     both(4, True)
-    far_signals()
-    x_direct_end()
-    use(6)
-    y_direct_end()
-    z_direct()
     use(3)
     use(7)
     use(4)
     finish_tokens()
-    z_direct_end()
+    z_direct_end(0)
+    z_direct_end(1)
     for copy in copies:
         copy.wait_send()
 
@@ -384,9 +404,9 @@
             pltpu.VMEM((1, ROWS // 4), F32),
             pltpu.VMEM((TOK, KV), BF16),
             pltpu.VMEM((TOK, LANE), F32),
-            pltpu.VMEM((NZL, 2 * TOK, ROWS), BF16),
-            pltpu.VMEM((NZL, ROWS, 2 * TOK), BF16),
-            pltpu.VMEM((2 * TOK, KV), BF16),
+            pltpu.VMEM((TOK, KV), BF16),
+            pltpu.VMEM((NZL, NX, NY, 8, KV), BF16),
+            pltpu.VMEM((NZL, NX, NY, 8, KV), BF16),
             pltpu.VMEM((NZL, NX, NY, 8, KV), F32),
             pltpu.VMEM((8, 2, ROWS, KV), BF16),
             pltpu.VMEM((NZL, TOK, 2 * ROWS), F32),
@@ -403,14 +423,13 @@
             pltpu.VMEM((NY - 1, NZL * 8, 2 * LANE), BF16),
             pltpu.VMEM((NY - 1, NZL * 8, 2 * LANE), BF16),
             pltpu.VMEM((NZL, 8, KV), F32),
-            pltpu.VMEM((2, NZL, 16, LANE), F32),
-            pltpu.VMEM((2, NZL, 16, LANE), BF16),
-            pltpu.VMEM((NZ - 1, 16, LANE), BF16),
+            pltpu.VMEM((2, 2, NZL, 8, LANE), F32),
+            pltpu.VMEM((2, 2, NZL, 8, LANE), BF16),
+            pltpu.VMEM((2, NZ - 1, 8, LANE), BF16),
             pltpu.SemaphoreType.DMA((N_SEM,)),
             pltpu.SemaphoreType.DMA((N_SEM,)),
             pltpu.SemaphoreType.DMA((16,)),
-            pltpu.SemaphoreType.REGULAR((2,)),
-            pltpu.SemaphoreType.REGULAR((2,)),
+            pltpu.SemaphoreType.REGULAR((3,)),
         ],
         compiler_params=pltpu.CompilerParams(
             collective_id=0, has_side_effects=True, vmem_limit_bytes=65_750_000

time: 55.7 us -> 53.9 us (0.968)
  the two profiles are of different devices: /device:TPU:6 before, /device:TPU:8 now
where the time goes in v3:
time: 53.9 us; the launch traced here: 53.7 us
  Pallas kernels  53.1 us (99%)
  between operations  0.64 us (1%)
    pallas_call x1, Pallas kernels, local(): pl.pallas_call(kernel, out_shape=tuple((OUT(*s) for s in shapes)), in_spe...  52 us

profile of v3, /device:TPU:8, one launch (start us, length us, event | category | flops | bytes accessed | tf_op | source)
XLA Modules:
  0.0 53.7 jit_solution(10591213746302775842)
XLA Ops:
  0.6 52.0 %key_projection.1 = (bf16[128,512]{1,0:T(8,128)(2,1)S(1)}, bf16[128,4096]{1,0:T(8,128)(2,1)S(1)}, f32[4,512]{1,0:T(4,128)S(1)}) custom-call(bf16[128,4096]{1,0:T(8,128)(2,1)} %tok_h.1, bf16[256,512]{1,0:T(8,128)(2,1)} %codes_h.1, f32[1,64]{1,0:T(1,128)} %bitcast.1, bf16[128,512]{1,0:T(8,128)(2,1)} %cot_h.1), custom_call_target="tpu_custom_call" | custom-call | tf_op jit(solution)/shard_map/key_projection/pallas_call | solution.py:396
  52.7 1.0 %put_out.1 = (bf16[128,512]{1,0:T(8,128)(2,1)}, bf16[128,4096]{1,0:T(8,128)(2,1)}, f32[4,512]{1,0:T(4,128)}) custom-call(bf16[128,512]{1,0:T(8,128)(2,1)S(1)} %get-tuple-element.6.keys, bf16[128,4096]{1,0:T(8,128)(2,1)S(1)} %get-tuple-element.7.grad_tokens, f32[4,512]{1,0:T(4,128)S(1)} %get-tuple-element.8.grad_weight), custom_call_target="tpu_custom_call" | custom-call | tf_op jit(solution)/shard_map/put_out/pallas_call | solution.py:439

commit v4 on v3

--- a/solution.py
+++ b/solution.py
@@ -152,7 +152,7 @@
             )
             return _
 
-        lax.fori_loop(0, NZL, rows, 0, unroll=2)
+        lax.fori_loop(0, NZL, rows, 0, unroll=4)
 
     def keep(b, v):
         part[b] = v
@@ -345,24 +345,24 @@
     both(1, True)
     use(0)
     hops("y", 2, True)
-    both(1, False)
     hops("x", 2, True)
     hops("y", 3, False)
+    both(1, False)
     know(1)
     hops("y", 3, True)
+    use(1)
+    hops("y", 4, False)
     both(2, True)
-    hops("y", 4, False)
-    use(1)
-    both(2, False)
     hops("y", 4, True)
     ring_end("x")
     y_direct()
+    both(2, False)
     use(5)
-    use(2)
-    both(3, True)
     ring_end("y")
     x_direct()
+    both(3, True)
     know(2)
+    use(2)
     use(6)
     x_direct_end()
     z_direct(0)
@@ -374,10 +374,10 @@
     use(7)
     use(4)
     finish_tokens()
+    for copy in copies:
+        copy.wait_send()
     z_direct_end(0)
     z_direct_end(1)
-    for copy in copies:
-        copy.wait_send()
 
 
 def put_out(keys, grad_tokens, grad_weight, keys_h, grad_tokens_h, grad_weight_h, sem):

time: 53.9 us -> 53.3 us (0.989)
  Pallas kernels: 53.1 us -> 52.5 us
    pallas_call x1, Pallas kernels: 52 us -> 51.4 us  [local(): pl.pallas_call(kernel, out_shape=tuple((OUT(*s) for s in shapes)), in_spe...]
where the time goes in v4:
time: 53.3 us; the launch traced here: 53.1 us
  Pallas kernels  52.5 us (98%)
  between operations  0.64 us (1%)
    pallas_call x1, Pallas kernels, local(): pl.pallas_call(kernel, out_shape=tuple((OUT(*s) for s in shapes)), in_spe...  51.4 us

profile of v4, /device:TPU:8, one launch (start us, length us, event | category | flops | bytes accessed | tf_op | source)
XLA Modules:
  0.0 53.1 jit_solution(2493635790888087225)
XLA Ops:
  0.6 51.4 %key_projection.1 = (bf16[128,512]{1,0:T(8,128)(2,1)S(1)}, bf16[128,4096]{1,0:T(8,128)(2,1)S(1)}, f32[4,512]{1,0:T(4,128)S(1)}) custom-call(bf16[128,4096]{1,0:T(8,128)(2,1)} %tok_h.1, bf16[256,512]{1,0:T(8,128)(2,1)} %codes_h.1, f32[1,64]{1,0:T(1,128)} %bitcast.1, bf16[128,512]{1,0:T(8,128)(2,1)} %cot_h.1), custom_call_target="tpu_custom_call" | custom-call | tf_op jit(solution)/shard_map/key_projection/pallas_call | solution.py:396
  52.1 1.0 %put_out.1 = (bf16[128,512]{1,0:T(8,128)(2,1)}, bf16[128,4096]{1,0:T(8,128)(2,1)}, f32[4,512]{1,0:T(4,128)}) custom-call(bf16[128,512]{1,0:T(8,128)(2,1)S(1)} %get-tuple-element.6.keys, bf16[128,4096]{1,0:T(8,128)(2,1)S(1)} %get-tuple-element.7.grad_tokens, f32[4,512]{1,0:T(4,128)S(1)} %get-tuple-element.8.grad_weight), custom_call_target="tpu_custom_call" | custom-call | tf_op jit(solution)/shard_map/put_out/pallas_call | solution.py:439
